TPU v7x, 32 devices: a whole 2x2x4 slice. The times are simulated.
32 devices in a mesh: dp: 8 (over z, y), tensor: 4 (over x, core).
Axes of the slice: x: 2, y: 2, z: 4, core: 2. Of those that a mesh axis runs over, the one named last changes fastest.
Arguments:
- tokens: bfloat16 [512, 1536], P('dp'), may hold values from -6 to 6
- norm_gain: float32 [1536], replicated, may hold values from 0.1 to 1.9
- w_query: bfloat16 [1536, 1024], P(None, 'tensor'), may hold values from -0.15625 to 0.15625
- w_keyval: bfloat16 [1536, 256], replicated, may hold values from -0.15625 to 0.15625
- w_out: bfloat16 [1024, 1536], P('tensor'), may hold values from -0.5 to 0.5
- kv_pool: bfloat16 [4096, 128, 256], P(('dp', 'tensor')), may hold values from -256 to 256
- page_table: int32 [512, 8], P('dp', 'tensor'), may hold values from 0 to 127, as said below
- positions: int32 [512], P('dp'), may hold values from 0 to 8191
- assignment: int32 [512], P('dp'), may hold values from 0 to 511, as said below
Outputs:
- attn_out: bfloat16 [512, 1536], P('dp')
Inputs may be any that keep to these rules, and one draw needn't show every extreme that they name: `assignment`: the serving slot is the serving device's dp index times 64 plus a local slot; each serving slot is taken by exactly one request; the 64 requests of one device go to 8 distinct devices, exactly 8 to each. `page_table`: on each device the entries form a permutation of 0 to 127.
All inputs are finite; a program needn't handle non-finite values.
Results may differ from a plain program's by a relative error of at most 0.03.
Values may be sent and summed in bfloat16 or wider, within the bound.
A program may use at most 64 MiB of HBM per device.

v0:
```python
import jax
import jax.numpy as jnp
from jax import lax
from jax.sharding import PartitionSpec as P

masked_score = -1e30
norm_eps = 1e-06
rotary_base = 10000.0


def combined_all(array, axis, join):
    gathered = jax.tree.map(
        lambda a, kind: lax.all_gather(a.astype(kind), axis),
        array,
        (jnp.bfloat16, jnp.bfloat16, jnp.bfloat16),
    )

    def take(source):
        return jax.tree.map(
            lambda a, own: lax.dynamic_index_in_dim(a, source, 0, False).astype(own.dtype),
            gathered,
            array,
        )

    return lax.fori_loop(
        1, lax.axis_size(axis), lambda source, state: join(state, take(source)), take(0)
    )


def as_sent(array):

    def short(part):
        return part.astype(jnp.bfloat16) if part.dtype == jnp.float32 else part

    return jax.tree.map(short, array)


def rotate(values, where, width):
    half = width // 2
    freqs = rotary_base ** (-jnp.arange(half, dtype=jnp.float32) * 2.0 / width)
    angles = where.astype(jnp.float32)[..., None] * freqs
    cosine = jnp.cos(angles)
    sine = jnp.sin(angles)
    first = values[..., :half]
    second = values[..., half:]
    return jnp.concatenate(
        [first * cosine - second * sine, first * sine + second * cosine], axis=-1
    )


def combine_stats(first, second):
    peak = jnp.maximum(first[0], second[0])
    first_scale = jnp.exp(first[0] - peak)
    second_scale = jnp.exp(second[0] - peak)
    total = first[1] * first_scale + second[1] * second_scale
    summed = first[2] * first_scale[..., None] + second[2] * second_scale[..., None]
    return (peak, total, summed)


def local(tokens, norm_gain, w_query, w_keyval, w_out, kv_pool, page_table, positions, assignment):
    head_width = w_keyval.shape[1] // 2
    row_count = tokens.shape[0]
    group_size = lax.axis_size("tensor")
    data_size = lax.axis_size("dp")
    local_heads = w_query.shape[1] // head_width
    all_heads = local_heads * group_size
    capacity = max(2, row_count // data_size)
    slots_all = data_size * capacity
    scale = head_width ** (-0.5)
    here = lax.axis_index("tensor")
    floats = tokens.astype(jnp.float32)
    normed = (
        floats * lax.rsqrt(jnp.mean(floats * floats, axis=-1, keepdims=True) + norm_eps) * norm_gain
    ).astype(jnp.bfloat16)
    query = jnp.dot(normed, w_query, preferred_element_type=jnp.float32).reshape(
        row_count, local_heads, head_width
    )
    query = rotate(query, positions[:, None], head_width).astype(jnp.bfloat16)
    key_value = jnp.dot(normed, w_keyval, preferred_element_type=jnp.float32)
    new_key = rotate(key_value[:, :head_width], positions, head_width).astype(jnp.bfloat16)
    new_value = key_value[:, head_width:].astype(jnp.bfloat16)
    target = assignment // row_count
    local_slot = assignment % row_count
    hits = (target[:, None] == jnp.arange(data_size, dtype=jnp.int32)[None, :]).astype(jnp.int32)
    order_in = jnp.sum(jnp.cumsum(hits, axis=0) * hits, axis=1) - 1
    place = target * capacity + order_in

    def to_buffer(values):
        empty = jnp.zeros((slots_all,) + values.shape[1:], values.dtype)
        filled = empty.at[place].set(values)
        return filled.reshape((data_size, capacity) + values.shape[1:])

    def source_buffer(values):
        return values.reshape((slots_all,) + values.shape[2:])[place]

    tags = to_buffer(jnp.stack([positions, local_slot + 1], axis=1))
    tags = lax.all_to_all(tags, "dp", split_axis=0, concat_axis=0, tiled=True).reshape(slots_all, 2)
    served_slot = tags[:, 1] - 1
    scatter_slot = jnp.where(served_slot < 0, row_count, served_slot)
    gather_slot = jnp.maximum(served_slot, 0)

    def compact(values):
        empty = jnp.zeros((row_count,) + values.shape[1:], values.dtype)
        return empty.at[scatter_slot].set(values, mode="drop")

    def expand(values):
        return values[gather_slot].reshape((data_size, capacity) + values.shape[1:])

    current = compact(tags[:, 0])
    full_query = lax.all_gather(query, "tensor", axis=1, tiled=True)
    served_heads = lax.all_to_all(
        to_buffer(full_query), "dp", split_axis=0, concat_axis=0, tiled=True
    )
    served_heads = compact(served_heads.reshape(slots_all, all_heads, head_width))
    page_rows = page_table.shape[1]
    page_len = kv_pool.shape[1]
    window = page_rows * group_size * page_len
    page_entries = kv_pool[page_table].reshape(row_count, page_rows * page_len, 2 * head_width)
    scores = (
        jnp.einsum(
            "vto,vio->vti",
            served_heads,
            page_entries[..., :head_width],
            preferred_element_type=jnp.float32,
        )
        * scale
    )
    cycle_slot = here * page_rows * page_len + jnp.arange(page_rows * page_len, dtype=jnp.int32)
    offset = jnp.mod(cycle_slot[None, :] - current[:, None], window)
    valid = ((offset != 0) & (current[:, None] - window + offset >= 0))[:, None, :]
    peak = jnp.max(jnp.where(valid, scores, masked_score), axis=2)
    weight_tensors = jnp.where(valid, jnp.exp(scores - peak[..., None]), 0.0)
    total = jnp.sum(weight_tensors, axis=2)
    summed = jnp.einsum(
        "rbi,ril->rbl",
        weight_tensors.astype(jnp.bfloat16),
        page_entries[..., head_width:],
        preferred_element_type=jnp.float32,
    )
    merged = combined_all((peak, total, summed), "tensor", combine_stats)
    returned = (
        lax.all_to_all(as_sent(expand(merged[0])), "dp", split_axis=0, concat_axis=0, tiled=True),
        lax.all_to_all(as_sent(expand(merged[1])), "dp", split_axis=0, concat_axis=0, tiled=True),
        lax.all_to_all(as_sent(expand(merged[2])), "dp", split_axis=0, concat_axis=0, tiled=True),
    )
    own_stats = tuple(
        (
            lax.dynamic_slice_in_dim(source_buffer(member), here * local_heads, local_heads, 1)
            for member in returned
        )
    )
    cache_peak, cache_total, cache_summed = own_stats
    self_score = (
        jnp.einsum("rhd,rd->rh", query, new_key, preferred_element_type=jnp.float32) * scale
    )
    overall = jnp.maximum(cache_peak, self_score)
    keep = jnp.exp(cache_peak - overall)
    fresh = jnp.exp(self_score - overall)
    full_total = cache_total * keep + fresh
    fresh_low = fresh.astype(jnp.bfloat16).astype(jnp.float32)
    full_summed = (
        cache_summed * keep[..., None]
        + fresh_low[..., None] * new_value.astype(jnp.float32)[:, None, :]
    )
    attended = (
        (full_summed / full_total[..., None])
        .astype(jnp.bfloat16)
        .reshape(row_count, local_heads * head_width)
    )
    partial_out = jnp.dot(attended, w_out, preferred_element_type=jnp.float32)
    return lax.psum(partial_out.astype(jnp.bfloat16), "tensor")


def solution(mesh):
    return jax.shard_map(
        local,
        mesh=mesh,
        in_specs=(
            P("dp", None),
            P(),
            P(None, "tensor"),
            P(),
            P("tensor", None),
            P(("dp", "tensor"), None, None),
            P("dp", "tensor"),
            P("dp"),
            P("dp"),
        ),
        out_specs=P("dp", None),
        check_vma=False,
    )
```

profile of v0, /device:TPU:0, one launch (start us, length us, event | category | flops | bytes accessed | tf_op | source)
XLA Modules:
  0.0 160.3 jit_solution(12733547716529152877)
XLA Ops:
  9.9 7.3 %all-to-all-start = ((s32[8,8,2]{1,2,0:T(2,128)}), s32[8,8,2]{1,2,0:T(2,128)S(1)}, u32[]{:S(2)}, u32[]{:S(2)}) async-start(s32[8,8,2]{1,2,0:T(2,128)} %copy.68), calls=%async_computation | async-start | bytes 16384 | tf_op jit(solution)/shard_map/all_to_all | solution.py:97
  19.9 1.6 fusion.25
  21.4 1.6 fusion.27
  23.8 5.4 %all_gather.17 = bf16[64,8,128]{2,0,1:T(8,128)(2,1)S(1)} all-gather(bf16[64,2,128]{2,0,1:T(8,128)(2,1)S(1)} %pad_maximum_fusion), channel_id=1, replica_groups=mesh['dp'=8,'tensor'=4] {'tensor'}, dimensions={1}, use_global_device_ids=true | all-gather | bytes 163840 | tf_op jit(solution)/shard_map/all_gather | solution.py:110
  30.0 6.9 %scatter_fusion = bf16[64,8,128]{2,1,0:T(8,128)(2,1)} fusion(bf16[64,8,128]{2,1,0:T(8,128)(2,1)} %broadcast.188.clone, s32[64]{0:T(128)S(1)} %compare_select_fusion.3, bf16[64,8,128]{2,1,0:T(8,128)(2,1)S(1)} %copy.72), kind=kCustom, calls=%fused_computation.9 | custom fusion | bytes 393472 | tf_op jit(solution)/shard_map/scatter | solution.py:90
  36.9 10.0 %gather_fusion = bf16[128,128,256]{2,1,0:T(8,128)(2,1)} fusion(bf16[128,128,256]{2,1,0:T(8,128)(2,1)} %param.16, s32[1024]{0:T(1024)S(1)} %pad_clamp_fusion.2), kind=kCustom, calls=%fused_computation | custom fusion | bytes 16777728 | tf_op jit(solution)/shard_map/gather | solution.py:118
  46.8 6.0 %all-to-all-start.1 = ((bf16[8,8,8,128]{3,2,1,0:T(8,128)(2,1)}), bf16[8,8,8,128]{3,2,1,0:T(8,128)(2,1)S(1)}, u32[]{:S(2)}, u32[]{:S(2)}) async-start(bf16[8,8,8,128]{3,2,1,0:T(8,128)(2,1)} %bitcast.9), calls=%async_computation.1 | async-start | bytes 262144 | tf_op jit(solution)/shard_map/all_to_all | solution.py:111
  53.8 6.5 %all-to-all-done.1 = bf16[8,8,8,128]{3,2,1,0:T(8,128)(2,1)S(1)} async-done(((bf16[8,8,8,128]{3,2,1,0:T(8,128)(2,1)}), bf16[8,8,8,128]{3,2,1,0:T(8,128)(2,1)S(1)}, u32[]{:S(2)}, u32[]{:S(2)}) %all-to-all-start.1) | async-done | bytes 131104 | tf_op jit(solution)/shard_map/all_to_all | solution.py:111
  60.3 2.5 %scatter_fusion.1 = bf16[64,8,128]{2,1,0:T(8,128)(2,1)S(1)} fusion(bf16[64,8,128]{2,1,0:T(8,128)(2,1)S(1)} %broadcast.188, s32[64]{0:T(128)S(1)} %get-tuple-element.216, bf16[64,8,128]{2,1,0:T(8,128)(2,1)S(1)} %bitcast.88), kind=kCustom, calls=%fused_computation.10 | custom fusion | bytes 393472 | tf_op jit(solution)/shard_map/scatter | solution.py:104
  62.8 3.5 %select_reduce_fusion = (f32[64,8]{1,0:T(8,128)S(1)}, f32[64,8,256]{2,1,0:T(8,128)S(1)}) fusion(pred[64,256]{1,0:T(8,128)(4,1)S(1)} %fusion.24, bf16[64,8,128]{2,1,0:T(8,128)(2,1)S(1)} %scatter_fusion.1, bf16[64,256,256]{2,1,0:T(8,128)(2,1)} %bitcast.82), kind=kOutput, calls=%fused_computation.27 | convolution fusion | flops 33947136 | bytes 4868096 | tf_op jit(solution)/shard_map/vto,vio->vti/dot_general | solution.py:120
  66.3 2.9 %fusion.10 = bf16[64,8,128]{2,1,0:T(8,128)(2,1)S(1)} fusion(bf16[64,256,256]{2,1,0:T(8,128)(2,1)} %bitcast.83, f32[64,8,256]{2,1,0:T(8,128)S(1)} %get-tuple-element.221, f32[64,8]{1,0:T(8,128)S(1)} %get-tuple-element.220, pred[64,256]{1,0:T(8,128)(4,1)S(1)} %fusion.24), kind=kOutput, calls=%fused_computation.25 | convolution fusion | flops 34013184 | bytes 4868096 | tf_op jit(solution)/shard_map/rbi,ril->rbl/dot_general | solution.py:134
  69.6 5.2 %all-gather.4 = bf16[4,64,8]{1,2,0:T(8,128)(2,1)S(1)} all-gather(bf16[1,64,8]{1,2,0:T(8,128)(2,1)S(1)} %copy.75), channel_id=3, replica_groups=mesh['dp'=8,'tensor'=4] {'tensor'}, dimensions={0}, use_global_device_ids=true | all-gather | bytes 5120 | tf_op jit(solution)/shard_map/all_gather | solution.py:13
  74.8 5.1 %all-gather.3 = bf16[4,64,8]{1,2,0:T(8,128)(2,1)S(1)} all-gather(bf16[1,64,8]{1,2,0:T(8,128)(2,1)S(1)} %copy.74), channel_id=2, replica_groups=mesh['dp'=8,'tensor'=4] {'tensor'}, dimensions={0}, use_global_device_ids=true | all-gather | bytes 5120 | tf_op jit(solution)/shard_map/all_gather | solution.py:13
  79.9 7.2 %all-gather.2 = bf16[256,8,128]{2,1,0:T(8,128)(2,1)S(1)} all-gather(bf16[64,8,128]{2,1,0:T(8,128)(2,1)S(1)} %fusion.10), channel_id=4, replica_groups=mesh['dp'=8,'tensor'=4] {'tensor'}, dimensions={0}, use_global_device_ids=true | all-gather | bytes 655360 | tf_op jit(solution)/shard_map/all_gather | solution.py:13
  87.2 1.5 while.19
  90.0 3.3 %all-to-all-start.3 = ((bf16[8,8,8]{2,1,0:T(8,128)(2,1)}), bf16[8,8,8]{2,1,0:T(8,128)(2,1)S(1)}, u32[]{:S(2)}, u32[]{:S(2)}) async-start(bf16[8,8,8]{2,1,0:T(8,128)(2,1)} %bitcast.65), calls=%async_computation.3 | async-start | bytes 32768 | tf_op jit(solution)/shard_map/all_to_all | solution.py:142
  94.7 5.2 %all-to-all-done.3 = bf16[8,8,8]{2,1,0:T(8,128)(2,1)S(1)} async-done(((bf16[8,8,8]{2,1,0:T(8,128)(2,1)}), bf16[8,8,8]{2,1,0:T(8,128)(2,1)S(1)}, u32[]{:S(2)}, u32[]{:S(2)}) %all-to-all-start.3) | async-done | bytes 1056 | tf_op jit(solution)/shard_map/all_to_all | solution.py:142
  99.9 3.3 %all-to-all-start.4 = ((bf16[8,8,8]{2,1,0:T(8,128)(2,1)}), bf16[8,8,8]{2,1,0:T(8,128)(2,1)S(1)}, u32[]{:S(2)}, u32[]{:S(2)}) async-start(bf16[8,8,8]{2,1,0:T(8,128)(2,1)} %bitcast.64), calls=%async_computation.4 | async-start | bytes 32768 | tf_op jit(solution)/shard_map/all_to_all | solution.py:143
  103.3 1.3 gather_fusion.1
  105.2 4.5 %all-to-all-done.4 = bf16[8,8,8]{2,1,0:T(8,128)(2,1)S(1)} async-done(((bf16[8,8,8]{2,1,0:T(8,128)(2,1)}), bf16[8,8,8]{2,1,0:T(8,128)(2,1)S(1)}, u32[]{:S(2)}, u32[]{:S(2)}) %all-to-all-start.4) | async-done | bytes 1056 | tf_op jit(solution)/shard_map/all_to_all | solution.py:143
  109.7 3.4 %all-to-all-start.2 = ((bf16[8,8,8,128]{3,2,1,0:T(8,128)(2,1)}), bf16[8,8,8,128]{3,2,1,0:T(8,128)(2,1)S(1)}, u32[]{:S(2)}, u32[]{:S(2)}) async-start(bf16[8,8,8,128]{3,2,1,0:T(8,128)(2,1)} %bitcast.18), calls=%async_computation.2 | async-start | bytes 262144 | tf_op jit(solution)/shard_map/all_to_all | solution.py:144
  114.4 6.0 %all-to-all-done.2 = bf16[8,8,8,128]{3,2,1,0:T(8,128)(2,1)S(1)} async-done(((bf16[8,8,8,128]{3,2,1,0:T(8,128)(2,1)}), bf16[8,8,8,128]{3,2,1,0:T(8,128)(2,1)S(1)}, u32[]{:S(2)}, u32[]{:S(2)}) %all-to-all-start.2) | async-done | bytes 131104 | tf_op jit(solution)/shard_map/all_to_all | solution.py:144
  122.3 29.6 %all-reduce.2.cloned.1.call-done = bf16[64,1536]{1,0:T(8,128)(2,1)} async-done(((bf16[64,1536]{1,0:T(8,128)(2,1)}), bf16[64,1536]{1,0:T(8,128)(2,1)}) %all-reduce.2.cloned.1.call-update) | async-done | bytes 196624 | tf_op jit(solution)/shard_map/psum | solution.py:171
  151.8 1.6 %copy.131 = bf16[64,1536]{1,0:T(8,128)(2,1)} copy(bf16[64,1536]{1,0:T(8,128)(2,1)} %all-reduce.2.cloned.1.call-done) | data formatting | bytes 393216
  (78 shorter events, 16.8 us)
Async XLA Ops:
  6.5 114.8 %copy-start = (bf16[256,1536]{1,0:T(8,128)(2,1)S(1)}, bf16[256,1536]{1,0:T(8,128)(2,1)}, u32[]{:S(2)}) copy-start(bf16[256,1536]{1,0:T(8,128)(2,1)} %param.15) | copy-start | bytes 2359300
  9.9 37.0 %all-to-all-start = ((s32[8,8,2]{1,2,0:T(2,128)}), s32[8,8,2]{1,2,0:T(2,128)S(1)}, u32[]{:S(2)}, u32[]{:S(2)}) async-start(s32[8,8,2]{1,2,0:T(2,128)} %copy.68), calls=%async_computation | async-start | bytes 16384 | tf_op jit(solution)/shard_map/all_to_all | solution.py:97
  46.8 13.5 %all-to-all-start.1 = ((bf16[8,8,8,128]{3,2,1,0:T(8,128)(2,1)}), bf16[8,8,8,128]{3,2,1,0:T(8,128)(2,1)S(1)}, u32[]{:S(2)}, u32[]{:S(2)}) async-start(bf16[8,8,8,128]{3,2,1,0:T(8,128)(2,1)} %bitcast.9), calls=%async_computation.1 | async-start | bytes 262144 | tf_op jit(solution)/shard_map/all_to_all | solution.py:111
  90.0 9.9 %all-to-all-start.3 = ((bf16[8,8,8]{2,1,0:T(8,128)(2,1)}), bf16[8,8,8]{2,1,0:T(8,128)(2,1)S(1)}, u32[]{:S(2)}, u32[]{:S(2)}) async-start(bf16[8,8,8]{2,1,0:T(8,128)(2,1)} %bitcast.65), calls=%async_computation.3 | async-start | bytes 32768 | tf_op jit(solution)/shard_map/all_to_all | solution.py:142
  99.9 9.9 %all-to-all-start.4 = ((bf16[8,8,8]{2,1,0:T(8,128)(2,1)}), bf16[8,8,8]{2,1,0:T(8,128)(2,1)S(1)}, u32[]{:S(2)}, u32[]{:S(2)}) async-start(bf16[8,8,8]{2,1,0:T(8,128)(2,1)} %bitcast.64), calls=%async_computation.4 | async-start | bytes 32768 | tf_op jit(solution)/shard_map/all_to_all | solution.py:143
  109.7 10.7 %all-to-all-start.2 = ((bf16[8,8,8,128]{3,2,1,0:T(8,128)(2,1)}), bf16[8,8,8,128]{3,2,1,0:T(8,128)(2,1)S(1)}, u32[]{:S(2)}, u32[]{:S(2)}) async-start(bf16[8,8,8,128]{3,2,1,0:T(8,128)(2,1)} %bitcast.18), calls=%async_computation.2 | async-start | bytes 262144 | tf_op jit(solution)/shard_map/all_to_all | solution.py:144
  113.1 38.7 %all-reduce.2.cloned.1.call-start = ((), (), s32[]{:S(2)}) async-start(), calls=%async_computation.5 | async-start | bytes 393216 | tf_op jit(solution)/shard_map/psum | solution.py:171
Sparse Core Ops, SparseCore 0:
  122.4 29.3 all-reduce.1
where the time goes:
time: 161 us; the launch traced here: 160 us
  waiting for transfers between devices  51.7 us (32%)
  local copies, waits for them, and re-layouts  31.7 us (20%)
  starting transfers between devices  23.4 us (15%)
  blocking collectives  23 us (14%)
  between operations  13.6 us (8%)
  matrix products  10.6 us (7%)
  other arithmetic  6.19 us (4%)
    psum x1, waiting for transfers between devices, local(): return lax.psum(partial_out.astype(jnp.bfloat16), 'tensor')  29.6 us
    all_gather x3, blocking collectives, combined_all(): lax.all_gather(a.astype(kind), axis)  17.6 us
    gather x1, local copies, waits for them, and re-layouts, local(): kv_pool[page_table].reshape(row_count, page_rows * page_len, 2 * head_width)  9.96 us
    scatter x2, local copies, waits for them, and re-layouts, to_buffer(): filled = empty.at[place].set(values)  7.66 us
    all_to_all x1, starting transfers between devices, local(): lax.all_to_all(tags, 'dp', split_axis=0, concat_axis=0, tiled=True)  7.28 us
    all_to_all x1, waiting for transfers between devices, local(): lax.all_to_all(to_buffer(full_query), 'dp', split_axis=0, concat_axis=0,...  6.47 us
    all_to_all x1, waiting for transfers between devices, local(): lax.all_to_all(as_sent(expand(merged[2])), 'dp', split_axis=0, concat_axi...  6.02 us
    all_to_all x1, starting transfers between devices, local(): lax.all_to_all(to_buffer(full_query), 'dp', split_axis=0, concat_axis=0,...  6 us
  transfers between devices with their start and end apart: 6, of which 5 were waited for; matrix products, arithmetic and copies ran while one was open for 19% of the time, Pallas kernels for 0%

commit v1 on v0

--- a/solution.py
+++ b/solution.py
@@ -168,7 +168,7 @@
         .reshape(row_count, local_heads * head_width)
     )
     partial_out = jnp.dot(attended, w_out, preferred_element_type=jnp.float32)
-    return lax.psum(partial_out.astype(jnp.bfloat16), "tensor")
+    return jnp.sum(lax.all_gather(partial_out.astype(jnp.bfloat16), "tensor"), axis=0)
 
 
 def solution(mesh):

time: 161 us -> 125 us (0.78)
  waiting for transfers between devices: 51.7 us -> 22.2 us
  between operations: 13.6 us -> 0.25 us
  blocking collectives: 23 us -> 31.6 us
  local copies, waits for them, and re-layouts: 31.7 us -> 30 us
    psum x1 -> x0, waiting for transfers between devices: 29.6 us -> none  [local(): return lax.psum(partial_out.astype(jnp.bfloat16), 'tensor')]
    all_gather x0 -> x1, blocking collectives: none -> 8.6 us  [local(): lax.all_gather(partial_out.astype(jnp.bfloat16), 'tensor')]
    unnamed x7 -> x6, local copies, waits for them, and re-layouts: 1.94 us -> 0.32 us
  transfers between devices with their start and end apart: 6 -> 5, of which waited for: 5 -> 4; matrix products, arithmetic and copies ran while one was open for 19% -> 24% of each run, Pallas kernels for 0% -> 0%
where the time goes in v1:
time: 125 us; the launch traced here: 124 us
  blocking collectives  31.6 us (25%)
  local copies, waits for them, and re-layouts  30 us (24%)
  starting transfers between devices  23.3 us (19%)
  waiting for transfers between devices  22.2 us (18%)
  matrix products  9.94 us (8%)
  other arithmetic  7 us (6%)
    all_gather x3, blocking collectives, combined_all(): lax.all_gather(a.astype(kind), axis)  17.6 us
    gather x1, local copies, waits for them, and re-layouts, local(): kv_pool[page_table].reshape(row_count, page_rows * page_len, 2 * head_width)  9.96 us
    all_gather x1, blocking collectives, local(): lax.all_gather(partial_out.astype(jnp.bfloat16), 'tensor')  8.6 us
    scatter x2, local copies, waits for them, and re-layouts, to_buffer(): filled = empty.at[place].set(values)  7.66 us
    all_to_all x1, starting transfers between devices, local(): lax.all_to_all(tags, 'dp', split_axis=0, concat_axis=0, tiled=True)  7.28 us
    all_to_all x1, waiting for transfers between devices, local(): lax.all_to_all(to_buffer(full_query), 'dp', split_axis=0, concat_axis=0,...  6.47 us
    all_to_all x1, waiting for transfers between devices, local(): lax.all_to_all(as_sent(expand(merged[2])), 'dp', split_axis=0, concat_axi...  6.06 us
    all_to_all x1, starting transfers between devices, local(): lax.all_to_all(to_buffer(full_query), 'dp', split_axis=0, concat_axis=0,...  6 us
  transfers between devices with their start and end apart: 5, of which 4 were waited for; matrix products, arithmetic and copies ran while one was open for 24% of the time, Pallas kernels for 0%

profile of v1, /device:TPU:0, one launch (start us, length us, event | category | flops | bytes accessed | tf_op | source)
XLA Modules:
  0.0 124.4 jit_solution(3898094773547497958)
XLA Ops:
  3.3 7.3 %all-to-all-start = ((s32[8,8,2]{1,2,0:T(2,128)}), s32[8,8,2]{1,2,0:T(2,128)S(1)}, u32[]{:S(2)}, u32[]{:S(2)}) async-start(s32[8,8,2]{1,2,0:T(2,128)} %copy.68), calls=%async_computation | async-start | bytes 16384 | tf_op jit(solution)/shard_map/all_to_all | solution.py:97
  13.3 1.6 %fusion.25 = f32[64,256]{1,0:T(8,128)S(1)} fusion(bf16[1536,256]{1,0:T(8,128)(2,1)} %param.14, bf16[64,1536]{1,0:T(8,128)(2,1)} %param.11, f32[1536]{0:T(1024)} %param.12, f32[64]{0:T(128)S(1)} %add_rsqrt_fusion), kind=kOutput, calls=%fused_computation.51 | convolution fusion | flops 50724864 | bytes 1054976 | tf_op jit(solution)/shard_map/dot_general | solution.py:79
  14.9 1.6 %fusion.27 = f32[64,256]{1,0:T(8,128)S(1)} fusion(bf16[1536,256]{1,0:T(8,128)(2,1)} %param.13, bf16[64,1536]{1,0:T(8,128)(2,1)} %param.11, f32[1536]{0:T(1024)} %param.12, f32[64]{0:T(128)S(1)} %add_rsqrt_fusion), kind=kOutput, calls=%fused_computation.52 | convolution fusion | flops 50724864 | bytes 1054976 | tf_op jit(solution)/shard_map/dot_general | solution.py:75
  17.2 5.4 %all_gather.23 = bf16[64,8,128]{2,0,1:T(8,128)(2,1)S(1)} all-gather(bf16[64,2,128]{2,0,1:T(8,128)(2,1)S(1)} %pad_maximum_fusion), channel_id=1, replica_groups=mesh['dp'=8,'tensor'=4] {'tensor'}, dimensions={1}, use_global_device_ids=true | all-gather | bytes 163840 | tf_op jit(solution)/shard_map/all_gather | solution.py:110
  23.4 6.9 %scatter_fusion = bf16[64,8,128]{2,1,0:T(8,128)(2,1)} fusion(bf16[64,8,128]{2,1,0:T(8,128)(2,1)} %broadcast.188.clone, s32[64]{0:T(128)S(1)} %compare_select_fusion.3, bf16[64,8,128]{2,1,0:T(8,128)(2,1)S(1)} %copy.72), kind=kCustom, calls=%fused_computation.9 | custom fusion | bytes 393472 | tf_op jit(solution)/shard_map/scatter | solution.py:90
  30.3 10.0 %gather_fusion = bf16[128,128,256]{2,1,0:T(8,128)(2,1)} fusion(bf16[128,128,256]{2,1,0:T(8,128)(2,1)} %param.16, s32[1024]{0:T(1024)S(1)} %pad_clamp_fusion.2), kind=kCustom, calls=%fused_computation | custom fusion | bytes 16777728 | tf_op jit(solution)/shard_map/gather | solution.py:118
  40.3 6.0 %all-to-all-start.1 = ((bf16[8,8,8,128]{3,2,1,0:T(8,128)(2,1)}), bf16[8,8,8,128]{3,2,1,0:T(8,128)(2,1)S(1)}, u32[]{:S(2)}, u32[]{:S(2)}) async-start(bf16[8,8,8,128]{3,2,1,0:T(8,128)(2,1)} %bitcast.9), calls=%async_computation.1 | async-start | bytes 262144 | tf_op jit(solution)/shard_map/all_to_all | solution.py:111
  47.3 6.5 %all-to-all-done.1 = bf16[8,8,8,128]{3,2,1,0:T(8,128)(2,1)S(1)} async-done(((bf16[8,8,8,128]{3,2,1,0:T(8,128)(2,1)}), bf16[8,8,8,128]{3,2,1,0:T(8,128)(2,1)S(1)}, u32[]{:S(2)}, u32[]{:S(2)}) %all-to-all-start.1) | async-done | bytes 131104 | tf_op jit(solution)/shard_map/all_to_all | solution.py:111
  53.8 2.5 %scatter_fusion.1 = bf16[64,8,128]{2,1,0:T(8,128)(2,1)S(1)} fusion(bf16[64,8,128]{2,1,0:T(8,128)(2,1)S(1)} %broadcast.188, s32[64]{0:T(128)S(1)} %get-tuple-element.216, bf16[64,8,128]{2,1,0:T(8,128)(2,1)S(1)} %bitcast.90), kind=kCustom, calls=%fused_computation.10 | custom fusion | bytes 393472 | tf_op jit(solution)/shard_map/scatter | solution.py:104
  56.3 3.5 %select_reduce_fusion = (f32[64,8]{1,0:T(8,128)S(1)}, f32[64,8,256]{2,1,0:T(8,128)S(1)}) fusion(pred[64,256]{1,0:T(8,128)(4,1)S(1)} %fusion.24, bf16[64,8,128]{2,1,0:T(8,128)(2,1)S(1)} %scatter_fusion.1, bf16[64,256,256]{2,1,0:T(8,128)(2,1)} %bitcast.83), kind=kOutput, calls=%fused_computation.27 | convolution fusion | flops 33947136 | bytes 4868096 | tf_op jit(solution)/shard_map/vto,vio->vti/dot_general | solution.py:120
  59.7 2.9 %fusion.10 = bf16[64,8,128]{2,1,0:T(8,128)(2,1)S(1)} fusion(bf16[64,256,256]{2,1,0:T(8,128)(2,1)} %bitcast.84, f32[64,8,256]{2,1,0:T(8,128)S(1)} %get-tuple-element.221, f32[64,8]{1,0:T(8,128)S(1)} %get-tuple-element.220, pred[64,256]{1,0:T(8,128)(4,1)S(1)} %fusion.24), kind=kOutput, calls=%fused_computation.25 | convolution fusion | flops 34013184 | bytes 4868096 | tf_op jit(solution)/shard_map/rbi,ril->rbl/dot_general | solution.py:134
  63.1 5.2 %all-gather.5 = bf16[4,64,8]{1,2,0:T(8,128)(2,1)S(1)} all-gather(bf16[1,64,8]{1,2,0:T(8,128)(2,1)S(1)} %copy.75), channel_id=3, replica_groups=mesh['dp'=8,'tensor'=4] {'tensor'}, dimensions={0}, use_global_device_ids=true | all-gather | bytes 5120 | tf_op jit(solution)/shard_map/all_gather | solution.py:13
  68.3 5.1 %all-gather.4 = bf16[4,64,8]{1,2,0:T(8,128)(2,1)S(1)} all-gather(bf16[1,64,8]{1,2,0:T(8,128)(2,1)S(1)} %copy.74), channel_id=2, replica_groups=mesh['dp'=8,'tensor'=4] {'tensor'}, dimensions={0}, use_global_device_ids=true | all-gather | bytes 5120 | tf_op jit(solution)/shard_map/all_gather | solution.py:13
  73.4 7.2 %all-gather.2 = bf16[256,8,128]{2,1,0:T(8,128)(2,1)S(1)} all-gather(bf16[64,8,128]{2,1,0:T(8,128)(2,1)S(1)} %fusion.10), channel_id=4, replica_groups=mesh['dp'=8,'tensor'=4] {'tensor'}, dimensions={0}, use_global_device_ids=true | all-gather | bytes 655360 | tf_op jit(solution)/shard_map/all_gather | solution.py:13
  80.7 1.5 %while.19 = (s32[]{:T(128)}, f32[64,8]{0,1:T(8,128)S(1)}, f32[64,8]{0,1:T(8,128)S(1)}, f32[64,8,128]{2,1,0:T(8,128)S(1)}, bf16[4,64,8]{1,2,0:T(8,128)(2,1)S(1)},...) while((s32[]{:T(128)}, f32[64,8]{0,1:T(8,128)S(1)}, ...), condition=%wide.region_10.11_spmd, body=%wide.region_9.10_spmd.sunk | while | flops 266245 | bytes 682127 | solution.py:25
  82.2 1.2 gather_fusion.3
  83.5 3.3 %all-to-all-start.3 = ((bf16[8,8,8]{2,1,0:T(8,128)(2,1)}), bf16[8,8,8]{2,1,0:T(8,128)(2,1)S(1)}, u32[]{:S(2)}, u32[]{:S(2)}) async-start(bf16[8,8,8]{2,1,0:T(8,128)(2,1)} %bitcast.66), calls=%async_computation.3 | async-start | bytes 32768 | tf_op jit(solution)/shard_map/all_to_all | solution.py:142
  88.2 5.2 %all-to-all-done.3 = bf16[8,8,8]{2,1,0:T(8,128)(2,1)S(1)} async-done(((bf16[8,8,8]{2,1,0:T(8,128)(2,1)}), bf16[8,8,8]{2,1,0:T(8,128)(2,1)S(1)}, u32[]{:S(2)}, u32[]{:S(2)}) %all-to-all-start.3) | async-done | bytes 1056 | tf_op jit(solution)/shard_map/all_to_all | solution.py:142
  93.3 3.3 %all-to-all-start.4 = ((bf16[8,8,8]{2,1,0:T(8,128)(2,1)}), bf16[8,8,8]{2,1,0:T(8,128)(2,1)S(1)}, u32[]{:S(2)}, u32[]{:S(2)}) async-start(bf16[8,8,8]{2,1,0:T(8,128)(2,1)} %bitcast.65), calls=%async_computation.4 | async-start | bytes 32768 | tf_op jit(solution)/shard_map/all_to_all | solution.py:143
  96.8 1.3 %gather_fusion.1 = bf16[64,8,128]{2,1,0:T(8,128)(2,1)} fusion(f32[64,8,128]{2,1,0:T(8,128)S(1)} %get-tuple-element.183, s32[1024]{0:T(1024)S(1)} %pad_clamp_fusion.1), kind=kCustom, calls=%fused_computation.1 | custom fusion | bytes 262400 | tf_op jit(solution)/shard_map/gather | solution.py:107
  98.7 4.5 %all-to-all-done.4 = bf16[8,8,8]{2,1,0:T(8,128)(2,1)S(1)} async-done(((bf16[8,8,8]{2,1,0:T(8,128)(2,1)}), bf16[8,8,8]{2,1,0:T(8,128)(2,1)S(1)}, u32[]{:S(2)}, u32[]{:S(2)}) %all-to-all-start.4) | async-done | bytes 1056 | tf_op jit(solution)/shard_map/all_to_all | solution.py:143
  103.2 3.4 %all-to-all-start.2 = ((bf16[8,8,8,128]{3,2,1,0:T(8,128)(2,1)}), bf16[8,8,8,128]{3,2,1,0:T(8,128)(2,1)S(1)}, u32[]{:S(2)}, u32[]{:S(2)}) async-start(bf16[8,8,8,128]{3,2,1,0:T(8,128)(2,1)} %bitcast.18), calls=%async_computation.2 | async-start | bytes 262144 | tf_op jit(solution)/shard_map/all_to_all | solution.py:144
  107.8 6.1 %all-to-all-done.2 = bf16[8,8,8,128]{3,2,1,0:T(8,128)(2,1)S(1)} async-done(((bf16[8,8,8,128]{3,2,1,0:T(8,128)(2,1)}), bf16[8,8,8,128]{3,2,1,0:T(8,128)(2,1)S(1)}, u32[]{:S(2)}, u32[]{:S(2)}) %all-to-all-start.2) | async-done | bytes 131104 | tf_op jit(solution)/shard_map/all_to_all | solution.py:144
  115.0 8.6 %all-gather.3 = bf16[256,1536]{1,0:T(8,128)(2,1)S(1)} all-gather(bf16[64,1536]{1,0:T(8,128)(2,1)S(1)} %convolution_convert_fusion), channel_id=5, replica_groups=mesh['dp'=8,'tensor'=4] {'tensor'}, dimensions={0}, use_global_device_ids=true | all-gather | bytes 983040 | tf_op jit(solution)/shard_map/all_gather | solution.py:171
  (76 shorter events, 15.6 us)
Async XLA Ops:
  0.0 114.8 %copy-start = (bf16[256,1536]{1,0:T(8,128)(2,1)S(1)}, bf16[256,1536]{1,0:T(8,128)(2,1)}, u32[]{:S(2)}) copy-start(bf16[256,1536]{1,0:T(8,128)(2,1)} %param.15) | copy-start | bytes 2359300
  3.3 36.9 %all-to-all-start = ((s32[8,8,2]{1,2,0:T(2,128)}), s32[8,8,2]{1,2,0:T(2,128)S(1)}, u32[]{:S(2)}, u32[]{:S(2)}) async-start(s32[8,8,2]{1,2,0:T(2,128)} %copy.68), calls=%async_computation | async-start | bytes 16384 | tf_op jit(solution)/shard_map/all_to_all | solution.py:97
  40.3 13.5 %all-to-all-start.1 = ((bf16[8,8,8,128]{3,2,1,0:T(8,128)(2,1)}), bf16[8,8,8,128]{3,2,1,0:T(8,128)(2,1)S(1)}, u32[]{:S(2)}, u32[]{:S(2)}) async-start(bf16[8,8,8,128]{3,2,1,0:T(8,128)(2,1)} %bitcast.9), calls=%async_computation.1 | async-start | bytes 262144 | tf_op jit(solution)/shard_map/all_to_all | solution.py:111
  83.5 9.9 %all-to-all-start.3 = ((bf16[8,8,8]{2,1,0:T(8,128)(2,1)}), bf16[8,8,8]{2,1,0:T(8,128)(2,1)S(1)}, u32[]{:S(2)}, u32[]{:S(2)}) async-start(bf16[8,8,8]{2,1,0:T(8,128)(2,1)} %bitcast.66), calls=%async_computation.3 | async-start | bytes 32768 | tf_op jit(solution)/shard_map/all_to_all | solution.py:142
  93.3 9.9 %all-to-all-start.4 = ((bf16[8,8,8]{2,1,0:T(8,128)(2,1)}), bf16[8,8,8]{2,1,0:T(8,128)(2,1)S(1)}, u32[]{:S(2)}, u32[]{:S(2)}) async-start(bf16[8,8,8]{2,1,0:T(8,128)(2,1)} %bitcast.65), calls=%async_computation.4 | async-start | bytes 32768 | tf_op jit(solution)/shard_map/all_to_all | solution.py:143
  103.2 10.7 %all-to-all-start.2 = ((bf16[8,8,8,128]{3,2,1,0:T(8,128)(2,1)}), bf16[8,8,8,128]{3,2,1,0:T(8,128)(2,1)S(1)}, u32[]{:S(2)}, u32[]{:S(2)}) async-start(bf16[8,8,8,128]{3,2,1,0:T(8,128)(2,1)} %bitcast.18), calls=%async_computation.2 | async-start | bytes 262144 | tf_op jit(solution)/shard_map/all_to_all | solution.py:144
